TPU v7x, 128 devices: a whole 4x4x4 slice. The times are simulated.
128 devices in a mesh: layer: 16 (over z_lo, x, core), lat: 8 (over z_hi, y).
Axes of the slice: x: 4, y: 4, z: 4 (z_hi: 2, z_lo: 2; z = z_hi * 2 + z_lo), core: 2. Of those that a mesh axis runs over, the one named last changes fastest.
Arguments:
- saved_codes: bfloat16 [16, 512, 1024], P('layer', 'lat'), may hold values from 0.049804688 to 2
- relu_mask: int32 [16, 512, 1024], P('layer', 'lat'), may hold values 0 or 1
- errors: bfloat16 [16, 1024, 4096], P('layer'), may hold values from -0.29882812 to 0.29882812
- decoders: bfloat16 [16, 16, 512, 4096], P('layer', None, 'lat'), may hold values from -0.59765625 to 0.59765625
- inputs: bfloat16 [16, 1024, 4096], P('layer'), may hold values from -0.3984375 to 0.3984375
Outputs:
- decoder_grad: bfloat16 [16, 16, 512, 4096], P('layer', None, 'lat')
- code_grad: float32 [16, 512, 1024], P('layer', 'lat')
- encoder_grad: bfloat16 [16, 512, 4096], P('layer', 'lat')
All inputs are finite; a program needn't handle non-finite values. No bound on the sum of `relu_mask` on one device may be relied on, other than what follows from the above.
Results may differ from a plain program's by a relative error of at most 0.0049.
Values may be sent and summed in bfloat16 or wider, within the bound.
No kernel may reach another device: no remote copies, remote signals or barrier semaphores. Data moves between devices by JAX's collectives and lax.ppermute only.
A program may use at most 128 MiB of HBM per device.

v0:
```python
import jax
import jax.numpy as jnp
from jax import lax
from jax.sharding import PartitionSpec as P


def body(saved_codes, relu_mask, errors, decoders, inputs):
    target = lax.axis_index("layer")
    target_error = errors[0]
    latents = saved_codes.shape[1]
    tokens = saved_codes.shape[2]
    model_width = target_error.shape[1]
    active = saved_codes * relu_mask.astype(jnp.bfloat16)
    gathered = lax.all_gather(active, "layer", axis=0, tiled=True)
    row_count = gathered.shape[0]
    allowed = (jnp.arange(row_count, dtype=jnp.int32) <= target)[:, None, None]

    def decoder_compute():
        products = jnp.dot(
            gathered.reshape(row_count * latents, tokens),
            target_error,
            preferred_element_type=jnp.float32,
        )
        products = products.reshape(row_count, latents, model_width)
        return jnp.where(allowed, products, 0.0).astype(jnp.bfloat16)

    def decoder_skipped():
        return jnp.zeros((row_count, latents, model_width), jnp.bfloat16)

    decoder_grad = lax.cond(jnp.int32(0) <= target, decoder_compute, decoder_skipped)
    code_row_count = 1 * lax.axis_size("layer")
    code_allowed = (jnp.arange(code_row_count, dtype=jnp.int32) <= target)[:, None, None]

    def code_compute():
        slab_rows = decoders[0]
        products = lax.dot_general(
            slab_rows.reshape(code_row_count * latents, model_width),
            target_error,
            (((1,), (1,)), ((), ())),
            preferred_element_type=jnp.float32,
        )
        products = products.reshape(code_row_count, latents, tokens)
        return jnp.where(code_allowed, products, 0.0)

    def code_skipped():
        return jnp.zeros((code_row_count, latents, tokens), jnp.float32)

    code_grad = lax.psum_scatter(
        lax.cond(jnp.int32(0) <= target, code_compute, code_skipped),
        "layer",
        scatter_dimension=0,
        tiled=True,
    )
    pre_grad = (code_grad[0] * relu_mask[0].astype(jnp.float32)).astype(jnp.bfloat16)
    encoder_grad = jnp.dot(pre_grad, inputs[0], preferred_element_type=jnp.float32).astype(
        jnp.bfloat16
    )
    return (decoder_grad[None], code_grad, encoder_grad[None])


def solution(mesh):
    return jax.shard_map(
        body,
        mesh=mesh,
        in_specs=(
            P("layer", "lat", None),
            P("layer", "lat", None),
            P("layer", None, None),
            P("layer", None, "lat", None),
            P("layer", None, None),
        ),
        out_specs=(P("layer", None, "lat", None), P("layer", "lat", None), P("layer", "lat", None)),
        check_vma=False,
    )
```

profile of v0, /device:TPU:0, one launch (start us, length us, event | category | flops | bytes accessed | tf_op | source)
XLA Modules:
  0.0 129.6 jit_solution(15806542635642984849)
XLA Ops:
  7.2 0.0 all-gather.2.cloned.1.call-start
  7.2 1.7 %convert_multiply_fusion = bf16[1,64,1024]{2,1,0:T(8,128)(2,1)} fusion(bf16[1,64,1024]{2,1,0:T(8,128)(2,1)} %param.9, s32[1,64,1024]{2,1,0:T(8,128)} %param.10), kind=kLoop, calls=%fused_computation.14 | loop fusion | flops 131072 | bytes 524288 | tf_op jit(solution)/shard_map/mul | solution.py:13
  8.9 0.0 all-gather.2.cloned.1.call-update
  8.9 0.0 reduce-scatter.2.cloned.1.call-start
  9.0 15.1 %conditional.3 = (f32[16,64,1024]{2,1,0:T(8,128)}) conditional(s32[]{:T(128)} %convert_element_type.23, () %tuple.24, (pred[16,1,1]{0,2,1:T(4,128)(4,1)S(1)}, bf16[1,16,64,4096]{3,2,1,0:T(8,128)(2,1)}, bf16[1024,4096]{1,0:T(8,128)(2,1)}) %tuple.35), branch_computations={%region_2.3_spmd, %region_3.4_spmd} | conditional | flops 8590983168 | bytes 20971544 | solution.py:49
  9.0 15.1 %broadcast_select_fusion = f32[16,64,1024]{2,1,0:T(8,128)} fusion(pred[16]{0:T(512)(128)(4,1)S(1)} %bitcast.35, bf16[1024,4096]{1,0:T(8,128)(2,1)} %get-tuple-element.24, bf16[1,16,64,4096]{3,2,1,0:T(8,128)(2,1)} %get-tuple-element.29), kind=kOutput, calls=%fused_computation.7 | convolution fusion | flops 8590983168 | bytes 20971536 | tf_op jit(solution)/shard_map/cond/branch_1_fun/dot_general | solution.py:36
  24.1 0.0 reduce-scatter.2.cloned.1.call-update
  24.1 22.5 %all-gather.2.cloned.1.call-done = bf16[16,64,1024]{2,1,0:T(8,128)(2,1)} async-done(((bf16[1,64,1024]{2,1,0:T(8,128)(2,1)}), bf16[16,64,1024]{2,1,0:T(8,128)(2,1)}) %all-gather.2.cloned.1.call-update) | async-done | bytes 2097168 | tf_op jit(solution)/shard_map/all_gather | solution.py:14
  46.6 0.0 copy-start
  46.6 14.8 %conditional.2 = (bf16[1,16,64,4096]{3,2,1,0:T(8,128)(2,1)}) conditional(s32[]{:T(128)} %convert_element_type.23, () %tuple.22, (pred[16,1,1]{0,2,1:T(4,128)(4,1)S(1)}, bf16[16,64,1024]{2,1,0:T(8,128)(2,1)}, bf16[1024,4096]{1,0:T(8,128)(2,1)}) %tuple.36), branch_computations={%region_0.0_spmd, %region_1.2_spmd} | conditional | flops 8598323200 | bytes 18874392 | solution.py:30
  46.6 14.8 %fusion = bf16[1,16,64,4096]{3,2,1,0:T(8,128)(2,1)} fusion(pred[16]{0:T(512)(128)(4,1)S(1)} %bitcast.36, bf16[16,64,1024]{2,1,0:T(8,128)(2,1)} %get-tuple-element.20, bf16[1024,4096]{1,0:T(8,128)(2,1)} %get-tuple-element.21), kind=kOutput, calls=%fused_computation.1 | convolution fusion | flops 8598323200 | bytes 18874384 | tf_op jit(solution)/shard_map/cond/branch_1_fun/dot_general | solution.py:19
  61.4 55.5 %reduce-scatter.2.cloned.1.call-done = f32[1,64,1024]{2,1,0:T(8,128)} async-done(((f32[16,64,1024]{2,1,0:T(8,128)}), f32[1,64,1024]{2,1,0:T(8,128)}) %reduce-scatter.2.cloned.1.call-update) | async-done | bytes 262160 | tf_op jit(solution)/shard_map/reduce_scatter | solution.py:48
  117.0 0.0 copy-done
  117.0 5.8 %fusion.17 = bf16[1,64,4096]{2,1,0:T(8,128)(2,1)} fusion(bf16[1,1024,4096]{2,1,0:T(8,128)(2,1)} %param.13, f32[1,64,1024]{2,1,0:T(8,128)} %reduce-scatter.2.cloned.1.call-done, s32[1,64,1024]{2,1,0:T(8,128)S(1)} %copy-done), kind=kOutput, calls=%fused_computation.11 | convolution fusion | flops 537329664 | bytes 9437184 | tf_op jit(solution)/shard_map/dot_general | solution.py:55
  (1 shorter events, 0.0 us)
Async XLA Ops:
  7.2 39.5 %all-gather.2.cloned.1.call-start = ((), (), s32[]{:S(2)}) async-start(), calls=%async_computation.1 | async-start | bytes 2228224 | tf_op jit(solution)/shard_map/all_gather | solution.py:14
  8.9 108.0 %reduce-scatter.2.cloned.1.call-start = ((), (), s32[]{:S(2)}) async-start(), calls=%async_computation.2 | async-start | bytes 4456448 | tf_op jit(solution)/shard_map/reduce_scatter | solution.py:48
  46.6 70.3 %copy-start = (s32[1,64,1024]{2,1,0:T(8,128)S(1)}, s32[1,64,1024]{2,1,0:T(8,128)}, u32[]{:S(2)}) copy-start(s32[1,64,1024]{2,1,0:T(8,128)} %param.10) | copy-start | bytes 786436
Sparse Core Ops, SparseCore 0:
  10.2 36.3 all-gather.1
  49.6 67.3 reduce-scatter.1
where the time goes:
time: 130 us
  waiting for transfers between devices  78.1 us (60%)
  matrix products  35.7 us (27%)
  between operations  14 us (11%)
  other arithmetic  1.71 us (1%)
    reduce_scatter x1, waiting for transfers between devices, body(): lax.psum_scatter(lax.cond(jnp.int32(0) <= target, code_compute, code_skip...  55.5 us
    all_gather x1, waiting for transfers between devices, body(): gathered = lax.all_gather(active, 'layer', axis=0, tiled=True)  22.5 us
    dot_general x1, matrix products, code_compute(): lax.dot_general(slab_rows.reshape(code_row_count * latents, model_width),...  15.1 us
    dot_general x1, matrix products, decoder_compute(): jnp.dot(gathered.reshape(row_count * latents, tokens), target_error, pref...  14.8 us
    dot_general x1, matrix products, body(): jnp.dot(pre_grad, inputs[0], preferred_element_type=jnp.float32)  5.84 us
  transfers between devices with their start and end apart: 2, of which 2 were waited for; matrix products, arithmetic and copies ran while one was open for 23% of the time, Pallas kernels for 0%

commit v1 on v0

--- a/solution.py
+++ b/solution.py
@@ -11,7 +11,9 @@
     tokens = saved_codes.shape[2]
     model_width = target_error.shape[1]
     active = saved_codes * relu_mask.astype(jnp.bfloat16)
-    gathered = lax.all_gather(active, "layer", axis=0, tiled=True)
+    gathered = jnp.concatenate(
+        lax.all_to_all(jnp.stack([active] * lax.axis_size("layer")), "layer", 0, 0), axis=0
+    )
     row_count = gathered.shape[0]
     allowed = (jnp.arange(row_count, dtype=jnp.int32) <= target)[:, None, None]
 

time: 130 us -> 119 us (0.915)
  waiting for transfers between devices: 78.1 us -> 61.5 us
  starting transfers between devices: 0.08 us -> 5.91 us
  other arithmetic: 1.71 us -> 0.03 us
  local copies, waits for them, and re-layouts: 0.01 us -> 1.59 us
    all_to_all x0 -> x1, waiting for transfers between devices: none -> 33.6 us  [body(): lax.all_to_all(jnp.stack([active] * lax.axis_size('layer')), 'layer', 0, 0)]
    reduce_scatter x1, waiting for transfers between devices: 55.5 us -> 27.9 us  [body(): lax.psum_scatter(lax.cond(jnp.int32(0) <= target, code_compute, code_skip...]
    all_gather x1 -> x0, waiting for transfers between devices: 22.5 us -> none  [body(): gathered = lax.all_gather(active, 'layer', axis=0, tiled=True)]
    all_to_all x0 -> x1, starting transfers between devices: none -> 5.87 us  [body(): lax.all_to_all(jnp.stack([active] * lax.axis_size('layer')), 'layer', 0, 0)]
    mul x1, other arithmetic: 1.7 us -> 0.02 us  [body(): active = saved_codes * relu_mask.astype(jnp.bfloat16)]
    another operation x0 -> x1, local copies, waits for them, and re-layouts: none -> 1.58 us  [body(): jnp.stack([active] * lax.axis_size('layer'))]
  transfers between devices with their start and end apart: 2 -> 2, of which waited for: 2 -> 2; matrix products, arithmetic and copies ran while one was open for 23% -> 14% of each run, Pallas kernels for 0% -> 0%
where the time goes in v1:
time: 119 us
  waiting for transfers between devices  61.5 us (52%)
  matrix products  35.4 us (30%)
  between operations  14.1 us (12%)
  starting transfers between devices  5.91 us (5%)
  local copies, waits for them, and re-layouts  1.59 us (1%)
    all_to_all x1, waiting for transfers between devices, body(): lax.all_to_all(jnp.stack([active] * lax.axis_size('layer')), 'layer', 0, 0)  33.6 us
    reduce_scatter x1, waiting for transfers between devices, body(): lax.psum_scatter(lax.cond(jnp.int32(0) <= target, code_compute, code_skip...  27.9 us
    dot_general x1, matrix products, code_compute(): lax.dot_general(slab_rows.reshape(code_row_count * latents, model_width),...  15.1 us
    dot_general x1, matrix products, decoder_compute(): jnp.dot(gathered.reshape(row_count * latents, tokens), target_error, pref...  14.5 us
    all_to_all x1, starting transfers between devices, body(): lax.all_to_all(jnp.stack([active] * lax.axis_size('layer')), 'layer', 0, 0)  5.87 us
    dot_general x1, matrix products, body(): jnp.dot(pre_grad, inputs[0], preferred_element_type=jnp.float32)  5.84 us
  transfers between devices with their start and end apart: 2, of which 2 were waited for; matrix products, arithmetic and copies ran while one was open for 14% of the time, Pallas kernels for 0%

profile of v1, /device:TPU:0, one launch (start us, length us, event | category | flops | bytes accessed | tf_op | source)
XLA Modules:
  0.0 118.6 jit_solution(13911508905482915515)
XLA Ops:
  7.2 0.0 reduce-scatter.2.cloned.1.call-start
  7.2 0.0 copy-start
  7.2 0.0 copy-start.1
  7.2 15.1 %conditional.3 = (f32[16,64,1024]{2,1,0:T(8,128)}) conditional(s32[]{:T(128)} %convert_element_type.23, () %tuple.24, (pred[16,1,1]{0,2,1:T(4,128)(4,1)S(1)}, bf16[1,16,64,4096]{3,2,1,0:T(8,128)(2,1)}, bf16[1024,4096]{1,0:T(8,128)(2,1)}) %tuple.34), branch_computations={%region_2.3_spmd, %region_3.4_spmd} | conditional | flops 8590983168 | bytes 20971544 | solution.py:51
  7.3 15.1 %broadcast_select_fusion = f32[16,64,1024]{2,1,0:T(8,128)} fusion(pred[16]{0:T(512)(128)(4,1)S(1)} %bitcast.40, bf16[1024,4096]{1,0:T(8,128)(2,1)} %get-tuple-element.24, bf16[1,16,64,4096]{3,2,1,0:T(8,128)(2,1)} %get-tuple-element.29), kind=kOutput, calls=%fused_computation.8 | convolution fusion | flops 8590983168 | bytes 20971536 | tf_op jit(solution)/shard_map/cond/branch_1_fun/dot_general | solution.py:38
  22.4 0.0 reduce-scatter.2.cloned.1.call-update
  22.4 0.0 copy-done
  22.4 0.0 copy-done.1
  22.4 1.6 %stack.2 = bf16[16,1,64,1024]{3,2,1,0:T(8,128)(2,1)} broadcast(bf16[64,1024]{1,0:T(8,128)(2,1)S(1)} %multiply_bitcast_fusion), dimensions={2,3} | broadcast | bytes 2228224 | tf_op jit(solution)/shard_map/stack | solution.py:15
  24.0 5.9 %all-to-all-start = ((bf16[16,1,64,1024]{3,2,1,0:T(8,128)(2,1)}), bf16[16,1,64,1024]{3,2,1,0:T(8,128)(2,1)S(1)}, u32[]{:S(2)}, u32[]{:S(2)}) async-start(bf16[16,1,64,1024]{3,2,1,0:T(8,128)(2,1)} %stack.2), calls=%async_computation | async-start | bytes 4194304 | tf_op jit(solution)/shard_map/all_to_all | solution.py:15
  29.9 33.6 %all-to-all-done = bf16[16,1,64,1024]{3,2,1,0:T(8,128)(2,1)S(1)} async-done(((bf16[16,1,64,1024]{3,2,1,0:T(8,128)(2,1)}), bf16[16,1,64,1024]{3,2,1,0:T(8,128)(2,1)S(1)}, u32[]{:S(2)}, u32[]{:S(2)}) %all-to-all-start) | async-done | bytes 2097184 | tf_op jit(solution)/shard_map/all_to_all | solution.py:15
  63.5 14.5 %conditional.2 = (bf16[1,16,64,4096]{3,2,1,0:T(8,128)(2,1)}) conditional(s32[]{:T(128)} %convert_element_type.23, () %tuple.22, (pred[16,1,1]{0,2,1:T(4,128)(4,1)S(1)}, bf16[16,1,64,1024]{3,2,1,0:T(8,128)(2,1)S(1)}, bf16[1024,4096]{1,0:T(8,128)(2,1)}) %tuple.35), branch_computations={%region_0.0_spmd, %region_1.2_spmd} | conditional | flops 8598323200 | bytes 18874392 | solution.py:32
  63.5 14.5 %fusion = bf16[1,16,64,4096]{3,2,1,0:T(8,128)(2,1)} fusion(pred[16]{0:T(512)(128)(4,1)S(1)} %bitcast.41, bf16[1024,4096]{1,0:T(8,128)(2,1)} %get-tuple-element.21, bf16[16,1,64,1024]{3,2,1,0:T(8,128)(2,1)S(1)} %get-tuple-element.31), kind=kOutput, calls=%fused_computation.1 | convolution fusion | flops 8598323200 | bytes 18874384 | tf_op jit(solution)/shard_map/cond/branch_1_fun/dot_general | solution.py:21
  78.0 27.9 %reduce-scatter.2.cloned.1.call-done = f32[1,64,1024]{2,1,0:T(8,128)} async-done(((f32[16,64,1024]{2,1,0:T(8,128)}), f32[1,64,1024]{2,1,0:T(8,128)}) %reduce-scatter.2.cloned.1.call-update) | async-done | bytes 262160 | tf_op jit(solution)/shard_map/reduce_scatter | solution.py:50
  105.9 5.8 %fusion.18 = bf16[1,64,4096]{2,1,0:T(8,128)(2,1)} fusion(bf16[1,1024,4096]{2,1,0:T(8,128)(2,1)} %param.13, f32[1,64,1024]{2,1,0:T(8,128)} %reduce-scatter.2.cloned.1.call-done, s32[1,64,1024]{2,1,0:T(8,128)S(1)} %copy-done), kind=kOutput, calls=%fused_computation.12 | convolution fusion | flops 537329664 | bytes 9437184 | tf_op jit(solution)/shard_map/dot_general | solution.py:57
  (2 shorter events, 0.0 us)
Async XLA Ops:
  7.2 98.7 %reduce-scatter.2.cloned.1.call-start = ((), (), s32[]{:S(2)}) async-start(), calls=%async_computation.2 | async-start | bytes 4456448 | tf_op jit(solution)/shard_map/reduce_scatter | solution.py:50
  7.2 15.2 %copy-start = (s32[1,64,1024]{2,1,0:T(8,128)S(1)}, s32[1,64,1024]{2,1,0:T(8,128)}, u32[]{:S(2)}) copy-start(s32[1,64,1024]{2,1,0:T(8,128)} %param.10) | copy-start | bytes 786436
  7.2 15.2 %copy-start.1 = (bf16[1,64,1024]{2,1,0:T(8,128)(2,1)S(1)}, bf16[1,64,1024]{2,1,0:T(8,128)(2,1)}, u32[]{:S(2)}) copy-start(bf16[1,64,1024]{2,1,0:T(8,128)(2,1)} %param.9) | copy-start | bytes 393220
  24.0 39.5 %all-to-all-start = ((bf16[16,1,64,1024]{3,2,1,0:T(8,128)(2,1)}), bf16[16,1,64,1024]{3,2,1,0:T(8,128)(2,1)S(1)}, u32[]{:S(2)}, u32[]{:S(2)}) async-start(bf16[16,1,64,1024]{3,2,1,0:T(8,128)(2,1)} %stack.2), calls=%async_computation | async-start | bytes 4194304 | tf_op jit(solution)/shard_map/all_to_all | solution.py:15
Sparse Core Ops, SparseCore 0:
  22.5 83.3 reduce-scatter.1
